TPU v7x, 768 devices: a whole 4x8x12 slice. The times are simulated.
768 devices in a mesh: seq: 96 (over z, x, core), head: 8 (over y).
Axes of the slice: x: 4, y: 8, z: 12, core: 2. Of those that a mesh axis runs over, the one named last changes fastest.
Arguments:
- queries: bfloat16 [24576, 4096], P('seq', 'head'), may hold values from -6 to 6
- key_vectors: bfloat16 [24576, 4096], P('seq', 'head'), may hold values from -0.5 to 0.5
- value_vectors: bfloat16 [24576, 4096], P('seq', 'head'), may hold values from -60 to 60
- out_grad: bfloat16 [24576, 4096], P('seq', 'head'), may hold values from -9.5 to 9.5
- norm_gain: float32 [4096], P('head'), may hold values from 0.1 to 1.9
Outputs:
- grad_queries: bfloat16 [24576, 4096], P('seq', 'head')
- grad_keys: bfloat16 [24576, 4096], P('seq', 'head')
- grad_values: bfloat16 [24576, 4096], P('seq', 'head')
- grad_gain: float32 [4096], P('head')
All inputs are finite; a program needn't handle non-finite values.
Results may differ from a plain program's by a relative error of at most 0.0049.
Values sent between devices are 32-bit elements; how exact they have to be, the bound alone decides.
A program may use at most 64 MiB of HBM per device.

v0:
```python
import jax
import jax.numpy as jnp
from jax import lax
from jax.sharding import PartitionSpec as P

DH = 128
BLOCK = 128


epsilon = 1e-06


def carried_in(part, axis, combine, identity, reverse):
    count = lax.axis_size(axis)
    place = lax.axis_index(axis)
    ahead = count - 1 - place if reverse else place
    gathered = lax.all_gather(part, axis)
    state = jnp.zeros_like(part) + jnp.asarray(identity, part.dtype)

    def one(step, state):
        source = count - 1 - step if reverse else step
        return combine(state, lax.dynamic_index_in_dim(gathered, source, 0, False))

    return lax.fori_loop(0, ahead, one, state)


def add_pair(first, second):
    return first + second


def exclusive_before(blocks):
    running = jnp.cumsum(blocks, axis=0)
    return jnp.concatenate([jnp.zeros_like(blocks[:1]), running[:-1]], axis=0)


def exclusive_after(blocks):
    running = jnp.cumsum(blocks[::-1], axis=0)[::-1]
    return jnp.concatenate([running[1:], jnp.zeros_like(blocks[:1])], axis=0)


def local(queries, key_vectors, value_vectors, out_grad, norm_gain):
    tok_rows = queries.shape[0]
    feature_count = queries.shape[1]
    head_count = feature_count // DH
    block_count = tok_rows // BLOCK
    block_shape = (block_count, BLOCK, head_count, DH)
    query_blocks = queries.reshape(block_shape)
    key_blocks = key_vectors.reshape(block_shape)
    value_blocks = value_vectors.reshape(block_shape)
    grad_f32 = out_grad.reshape(block_shape).astype(jnp.float32)
    gain_heads = norm_gain.reshape(head_count, DH)
    causal = (jnp.arange(BLOCK)[:, None] >= jnp.arange(BLOCK)[None, :])[None, None]
    high = lax.Precision.HIGHEST
    float_type = jnp.float32
    products = jnp.einsum(
        "bthd,bshd->bhts", query_blocks, key_blocks, preferred_element_type=float_type
    )
    scores = jnp.where(causal, products, 0.0).astype(jnp.bfloat16)
    key_value = jnp.einsum(
        "bshd,bshe->bhde", key_blocks, value_blocks, preferred_element_type=float_type
    )
    shard_total = jnp.sum(key_value, axis=0)
    earlier = carried_in(shard_total, "seq", add_pair, jnp.zeros_like(shard_total), False)
    states = earlier[None] + exclusive_before(key_value)
    attention = jnp.einsum(
        "bhts,bshe->bthe", scores, value_blocks, preferred_element_type=float_type
    )
    attention = attention + jnp.einsum(
        "bthd,bhde->bthe", query_blocks.astype(float_type), states, precision=high
    )
    square_part = jnp.sum(attention * attention, axis=(2, 3))
    weighted_part = jnp.sum(gain_heads * grad_f32 * attention, axis=(2, 3))
    square_sum, weighted = lax.psum((square_part, weighted_part), "head")
    model_width = feature_count * lax.axis_size("head")
    inverse_rms = (1.0 / jnp.sqrt(square_sum / model_width + epsilon))[:, :, None, None]
    gain_part = jnp.sum(grad_f32 * attention * inverse_rms, axis=(0, 1))
    grad_attention = gain_heads * grad_f32 * inverse_rms
    grad_attention = grad_attention - attention * (
        inverse_rms**3 * weighted[:, :, None, None] / model_width
    )
    grad_attention = grad_attention.astype(jnp.bfloat16)
    query_grad = jnp.einsum(
        "bthd,bthe->bhde", query_blocks, grad_attention, preferred_element_type=float_type
    )
    shard_grad = jnp.sum(query_grad, axis=0)
    after = carried_in(shard_grad, "seq", add_pair, jnp.zeros_like(shard_grad), True)
    grad_gain = lax.psum(gain_part, "seq")
    later = after[None] + exclusive_after(query_grad)
    grad_products = jnp.einsum(
        "bthe,bshe->bhts", grad_attention, value_blocks, preferred_element_type=float_type
    )
    grad_scores = jnp.where(causal, grad_products, 0.0).astype(jnp.bfloat16)
    attention_wide = grad_attention.astype(float_type)
    grad_query = jnp.einsum(
        "bhts,bshd->bthd", grad_scores, key_blocks, preferred_element_type=float_type
    )
    grad_query = grad_query + jnp.einsum("bthe,bhde->bthd", attention_wide, states, precision=high)
    grad_key = jnp.einsum(
        "bhts,bthd->bshd", grad_scores, query_blocks, preferred_element_type=float_type
    )
    grad_key = grad_key + jnp.einsum(
        "bshe,bhde->bshd", value_blocks.astype(float_type), later, precision=high
    )
    grad_value = jnp.einsum(
        "bhts,bthe->bshe", scores, grad_attention, preferred_element_type=float_type
    )
    grad_value = grad_value + jnp.einsum(
        "bshd,bhde->bshe", key_blocks.astype(float_type), later, precision=high
    )
    flat_shape = (tok_rows, feature_count)
    return (
        grad_query.reshape(flat_shape).astype(jnp.bfloat16),
        grad_key.reshape(flat_shape).astype(jnp.bfloat16),
        grad_value.reshape(flat_shape).astype(jnp.bfloat16),
        grad_gain.reshape(feature_count),
    )


def solution(mesh):
    in_specs = (P("seq", "head"), P("seq", "head"), P("seq", "head"), P("seq", "head"), P("head"))
    out_specs = (P("seq", "head"), P("seq", "head"), P("seq", "head"), P("head"))
    return jax.shard_map(local, mesh=mesh, in_specs=in_specs, out_specs=out_specs, check_vma=False)
```

profile of v0, /device:TPU:1, one launch (start us, length us, event | category | flops | bytes accessed | tf_op | source)
XLA Modules:
  0.0 601.8 jit_solution(13824844256623208957)
XLA Ops:
  7.2 1.0 reshape.52
  8.2 1.0 reshape.51
  10.6 1.0 reshape.50
  11.6 1.1 reshape.54
  13.3 162.0 %all-gather.5.cloned.1.call-done = f32[384,128,128]{2,1,0:T(8,128)} async-done(((f32[4,128,128]{2,1,0:T(8,128)}), f32[384,128,128]{2,1,0:T(8,128)}) %all-gather.5.cloned.1.call-update) | async-done | bytes 25165840 | tf_op jit(solution)/shard_map/all_gather | solution.py:17
  175.3 1.0 while.22
  177.3 13.2 %psum.21 = f32[2,128]{1,0:T(2,128)S(1)} all-reduce(f32[2,128]{1,0:T(2,128)S(1)} %get-tuple-element.105), channel_id=1, replica_groups=mesh['seq'=96,'head'=8] {'head'}, use_global_device_ids=true, to_apply=%region_5.6 | all-reduce | flops 256 | bytes 2048 | tf_op jit(solution)/shard_map/psum | solution.py:73
  191.5 11.5 %psum.22 = f32[2,128]{1,0:T(2,128)S(1)} all-reduce(f32[2,128]{1,0:T(2,128)S(1)} %get-tuple-element.86), channel_id=1, replica_groups=mesh['seq'=96,'head'=8] {'head'}, use_global_device_ids=true, to_apply=%region_7.8 | all-reduce | flops 256 | bytes 2048 | tf_op jit(solution)/shard_map/psum | solution.py:73
  203.8 1.0 fusion.31
  207.1 287.5 %psum.23 = f32[512]{0:T(512)} all-reduce(f32[512]{0:T(512)S(1)} %bitcast.71), channel_id=1, replica_groups=mesh['seq'=96,'head'=8] {'seq'}, use_global_device_ids=true, to_apply=%region_13.14 | all-reduce | flops 512 | bytes 4096 | tf_op jit(solution)/shard_map/psum | solution.py:87
  494.6 97.1 %while.23 = (s32[]{:T(128)}, f32[4,128,128]{2,1,0:T(8,128)S(1)}, s32[]{:T(128)}, f32[96,4,128,128]{3,2,1,0:T(8,128)}, s32[]{:T(128)}, /*index=5*/s32[]{:T(128)}, s32[]{:T(128)}, s32[]{:T(128)}) while((s32[]{:T(128)}, f32[4,128,128]{2,1,0:T(8,128)S(1)}, s32[]{:T(128)}, f32[96,4,128,128]{3,2,1,0:T(8,128)}, s32[]{:T(128)}, ...), condition=%wide.region_10.11_spmd, body=%wide.region_9.10_spmd.sunk | while | flops 65542 | bytes 786575 | solution.py:24
  500.9 1.0 bitcast_add_fusion.5
  501.9 1.0 bitcast_add_fusion.5
  502.9 1.0 bitcast_add_fusion.5
  511.2 1.0 bitcast_add_fusion.5
  512.2 1.0 bitcast_add_fusion.5
  513.3 1.0 bitcast_add_fusion.5
  520.5 1.0 bitcast_add_fusion.5
  521.5 1.0 bitcast_add_fusion.5
  522.6 1.0 bitcast_add_fusion.5
  530.8 1.0 bitcast_add_fusion.5
  531.9 1.0 bitcast_add_fusion.5
  532.9 1.0 bitcast_add_fusion.5
  540.1 1.0 bitcast_add_fusion.5
  (117 shorter events, 92.9 us)
Async XLA Ops:
  7.2 584.6 %copy-start = (pred[2]{0:T(512)(128)(4,1)S(1)}, pred[2]{0:T(512)(128)(4,1)}, u32[]{:S(2)}) copy-start(pred[2]{0:T(512)(128)(4,1)} %constant.58.clone.1) | copy-start | bytes 10
  7.2 168.1 %all-gather.5.cloned.1.call-start = ((), (), s32[]{:S(2)}) async-start(), calls=%async_computation | async-start | bytes 25427968 | tf_op jit(solution)/shard_map/all_gather | solution.py:17
  10.3 484.3 %all-gather.7.cloned.1.call-start = ((), (), s32[]{:S(2)}) async-start(), calls=%async_computation.1 | async-start | bytes 25427968 | tf_op jit(solution)/shard_map/all_gather | solution.py:17
Sparse Core Ops, SparseCore 0:
  12.3 162.9 all-gather.4
  205.0 248.8 all-gather.6
where the time goes:
time: 605 us; the launch traced here: 602 us
  blocking collectives  312 us (52%)
  waiting for transfers between devices  162 us (27%)
  other arithmetic  98.1 us (16%)
  between operations  14.2 us (2%)
  local copies, waits for them, and re-layouts  6.66 us (1%)
  matrix products  6.28 us (1%)
    psum x1, blocking collectives, local(): grad_gain = lax.psum(gain_part, 'seq')  288 us
    all_gather x2, waiting for transfers between devices, carried_in(): gathered = lax.all_gather(part, axis)  162 us
    add x95, other arithmetic, add_pair(): return first + second  96 us
    psum x2, blocking collectives, local(): square_sum, weighted = lax.psum((square_part, weighted_part), 'head')  24.7 us
  transfers between devices with their start and end apart: 2, of which 1 were waited for; matrix products, arithmetic and copies ran while one was open for 1% of the time, Pallas kernels for 0%

commit v1 on v0

v1 whole, which is shorter than its diff:
```python
import functools

import jax
import jax.numpy as jnp
from jax import lax
from jax.experimental import pallas as pl
from jax.experimental.pallas import tpu as pltpu
from jax.sharding import PartitionSpec as P

DH = 128
BLOCK = 128
PLANE = 8
NEAR = (1, 2, 3)
FAR = (4, 8)
EPSILON = 1e-06
MESH = pl.DeviceIdType.MESH
F32 = jnp.float32
BF16 = jnp.bfloat16


def dot(left, right, left_dim, right_dim):
    return lax.dot_general(
        left, right, (((left_dim,), (right_dim,)), ((), ())), preferred_element_type=F32
    )


def split(wide):
    high = wide.astype(BF16)
    low = (wide - high.astype(F32)).astype(BF16)
    return high, low


def dot_wide(left, wide, wide_dim):
    high, low = split(wide)
    return dot(left, high, 1, wide_dim) + dot(left, low, 1, wide_dim)


def kernel(
    z_count, y_count, head_count, block_count,
    q_ref, k_ref, v_ref, g_ref, gain_ref,
    gq_ref, gk_ref, gv_ref, gg_ref,
    inner, att, scores, grad_att, gk_part, gv_part, earlier, later,
    total_f, plane_f, step_f, near_f, window_f, far_f, stage_f,
    total_b, plane_b, step_b, near_b, window_b, far_b, stage_b,
    sums,
    fa_send, fa_recv, fb_send, fb_recv, fc_send, fc_recv,
    ba_send, ba_recv, bb_send, bb_recv, bc_send, bc_recv,
    h_send, h_recv,
):
    seq = lax.axis_index("seq")
    y = lax.axis_index("head")
    z = lax.div(seq, PLANE)
    p = lax.rem(seq, PLANE)
    piece = head_count * DH // PLANE
    model_width = y_count * head_count * DH

    def in_plane(offset):
        return lax.rem(p + offset, PLANE)

    def in_column(offset):
        return lax.rem(z + offset, z_count)

    def seq_of(at_z, at_p):
        return at_z * PLANE + at_p

    hops = sorted({d % z_count for d in NEAR + FAR} | {-d % z_count for d in NEAR + FAR})
    barrier = pltpu.get_barrier_semaphore()
    for k in range(1, PLANE):
        pl.semaphore_signal(barrier, inc=1, device_id=(seq_of(z, in_plane(k)), y), device_id_type=MESH)
    for d in hops:
        pl.semaphore_signal(barrier, inc=1, device_id=(seq_of(in_column(d), p), y), device_id_type=MESH)
    for k in range(1, y_count):
        pl.semaphore_signal(barrier, inc=1, device_id=(seq, lax.rem(y + k, y_count)), device_id_type=MESH)

    def remote(source, target, send, recv, seq_to, y_to):
        return pltpu.make_async_remote_copy(
            src_ref=source, dst_ref=target, send_sem=send, recv_sem=recv,
            device_id=(seq_to, y_to), device_id_type=MESH,
        )

    def plane_out(total, plane, send, recv):
        copies = []
        for k in (4, 3, 5, 2, 6, 1, 7):
            to = in_plane(k)
            copy = remote(total.at[to], plane.at[k], send.at[k], recv.at[k], seq_of(z, to), y)
            copy.start()
            copies.append(copy)
        return copies

    def column_out(source, slots, send, recv, distances, sign):
        copies = []
        for d in reversed(distances):
            to = in_column((sign * d) % z_count)
            at = (NEAR + FAR).index(d)
            copy = remote(
                source, slots.at[distances.index(d)], send.at[at], recv.at[at], seq_of(to, p), y
            )
            copy.start()
            copies.append(copy)
        return copies

    def plane_back(stage, target, send, recv):
        copies = []
        for k in (4, 3, 5, 2, 6, 1, 7):
            to = in_plane(k)
            copy = remote(stage.at[to], target.at[p], send.at[k], recv.at[k], seq_of(z, to), y)
            copy.start()
            copies.append(copy)
        return copies

    def finish(copies):
        for copy in copies:
            copy.wait()

    def plane_sum(total, plane):
        value = total[p]
        for k in range(1, PLANE):
            value = value + plane[k]
        return value

    def reached(d, reverse):
        return (z + d < z_count) if reverse else (z >= d)

    def gated(value, d, reverse):
        state = jnp.where(reached(d, reverse), value[:piece], 0.0)
        if value.shape[0] == piece:
            return state
        return jnp.concatenate([state, value[piece:]], axis=0)

    def stages(carried, total, plane, stage, reverse):
        for target in range(PLANE):
            value = carried
            for k in range(PLANE):
                source = lax.rem(p + PLANE - k, PLANE)
                part = (total[p] if k == 0 else plane[k])[:piece]
                wanted = (source > target) if reverse else (source < target)
                value = value + jnp.where(wanted, part, 0.0)
            stage[target] = value

    row = lax.broadcasted_iota(jnp.int32, (BLOCK, BLOCK), 0)
    col = lax.broadcasted_iota(jnp.int32, (BLOCK, BLOCK), 1)
    causal = row >= col

    def at(ref, b, h):
        return ref[b * BLOCK : (b + 1) * BLOCK, h * DH : (h + 1) * DH]

    def cols(h):
        return slice(h * DH, (h + 1) * DH)

    half = DH // piece

    def put_total(total, h, value):
        for i in range(half):
            total[h * half + i, 0:piece] = value[i * piece : (i + 1) * piece]

    def carried_state(ref, h):
        return jnp.concatenate([ref[h * half + i] for i in range(half)], axis=0)

    for h in range(head_count):
        first = dot(at(k_ref, 0, h), at(v_ref, 0, h), 0, 0)
        second = dot(at(k_ref, 1, h), at(v_ref, 1, h), 0, 0)
        inner[h] = first
        put_total(total_f, h, first + second)

    pl.semaphore_wait(barrier, PLANE - 1 + len(hops) + y_count - 1)
    sent = plane_out(total_f, plane_f, fa_send, fa_recv)

    for h in range(head_count):
        for b in range(block_count):
            products = dot(at(q_ref, b, h), at(k_ref, b, h), 1, 1)
            kept = jnp.where(causal, products, 0.0).astype(BF16)
            scores[b * BLOCK : (b + 1) * BLOCK, cols(h)] = kept
            value = dot(kept, at(v_ref, b, h), 1, 0)
            if b == 1:
                value = value + dot_wide(at(q_ref, b, h), inner[h], 0)
            att[b * BLOCK : (b + 1) * BLOCK, cols(h)] = value

    def scan(total, plane, step, near, window, far, stage, target, sems, sent, reverse):
        b_send, b_recv, c_send, c_recv = sems
        sign = -1 if reverse else 1
        finish(sent)
        step[...] = plane_sum(total, plane)
        sent = column_out(step, near, b_send, b_recv, NEAR, sign)
        finish(sent)
        before = gated(near[0], NEAR[0], reverse)
        for i in range(1, len(NEAR)):
            before = before + gated(near[i], NEAR[i], reverse)
        window[...] = before + step[...]
        sent = column_out(window, far, b_send, b_recv, FAR, sign)
        finish(sent)
        carried = before[:piece]
        for i in range(len(FAR)):
            carried = carried + gated(far[i], FAR[i], reverse)[:piece]
        stages(carried, total, plane, stage, reverse)
        sent = plane_back(stage, target, c_send, c_recv)
        target[p] = stage[p]
        return sent

    sent = scan(
        total_f, plane_f, step_f, near_f, window_f, far_f, stage_f, earlier,
        (fb_send, fb_recv, fc_send, fc_recv), sent, False,
    )
    finish(sent)

    squares = jnp.zeros((block_count * BLOCK, DH), F32)
    weighted = jnp.zeros((block_count * BLOCK, DH), F32)
    for h in range(head_count):
        value = att[:, cols(h)] + dot_wide(q_ref[:, cols(h)], carried_state(earlier, h), 0)
        att[:, cols(h)] = value
        squares = squares + value * value
        weighted = weighted + gain_ref[:, cols(h)] * g_ref[:, cols(h)].astype(F32) * value
    tokens = block_count * BLOCK
    square_row = jnp.sum(squares.T, axis=0, keepdims=True)
    weighted_row = jnp.sum(weighted.T, axis=0, keepdims=True)
    line = lax.broadcasted_iota(jnp.int32, (8, tokens), 0)
    sums[0] = jnp.where(line == 0, square_row, jnp.where(line == 1, weighted_row, 0.0))
    sent = []
    for k in (4, 3, 5, 2, 6, 1, 7):
        copy = remote(sums.at[0], sums.at[k], h_send.at[k], h_recv.at[k], seq, lax.rem(y + k, y_count))
        copy.start()
        sent.append(copy)
    finish(sent)
    whole = sums[0]
    for k in range(1, y_count):
        whole = whole + sums[k]
    inverse_row = 1.0 / jnp.sqrt(whole[0:1] / model_width + EPSILON)
    pull_row = inverse_row * inverse_row * inverse_row * whole[1:2] / model_width
    inverse = jnp.broadcast_to(inverse_row, (DH, tokens)).T
    pull = jnp.broadcast_to(pull_row, (DH, tokens)).T

    gain_line = lax.broadcasted_iota(jnp.int32, (8, DH), 0)
    gain_part = jnp.zeros((8, DH), F32)
    for h in range(head_count):
        value = att[:, cols(h)]
        scaled = g_ref[:, cols(h)].astype(F32) * inverse
        gain_sum = jnp.sum(scaled * value, axis=0, keepdims=True)
        gain_part = jnp.where(gain_line == h, gain_sum, gain_part)
        grad = (gain_ref[:, cols(h)] * scaled - value * pull).astype(BF16)
        grad_att[:, cols(h)] = grad
        first = dot(at(q_ref, 0, h), grad[:BLOCK], 0, 0)
        second = dot(at(q_ref, 1, h), grad[BLOCK:], 0, 0)
        inner_b = second
        att[0:DH, cols(h)] = inner_b
        put_total(total_b, h, first + second)
    for s in range(PLANE):
        total_b[s, piece : piece + 8] = gain_part
    sent = plane_out(total_b, plane_b, ba_send, ba_recv)

    for h in range(head_count):
        state = carried_state(earlier, h)
        after_first = att[0:DH, cols(h)]
        for b in range(block_count):
            rows = slice(b * BLOCK, (b + 1) * BLOCK)
            grad = grad_att[rows, cols(h)]
            products = dot(grad, at(v_ref, b, h), 1, 1)
            grad_scores = jnp.where(causal, products, 0.0).astype(BF16)
            here = state + inner[h] if b == 1 else state
            value = dot(grad_scores, at(k_ref, b, h), 1, 0) + dot_wide(grad, here, 1)
            gq_ref[rows, cols(h)] = value.astype(BF16)
            key = dot(grad_scores, at(q_ref, b, h), 0, 0)
            val = dot(scores[rows, cols(h)], grad, 0, 0)
            if b == 0:
                key = key + dot_wide(at(v_ref, b, h), after_first, 1)
                val = val + dot_wide(at(k_ref, b, h), after_first, 0)
            gk_part[rows, cols(h)] = key
            gv_part[rows, cols(h)] = val

    sent = scan(
        total_b, plane_b, step_b, near_b, window_b, far_b, stage_b, later,
        (bb_send, bb_recv, bc_send, bc_recv), sent, True,
    )
    gg_ref[...] = window_b[piece : piece + 8] + far_b[0, piece : piece + 8] + far_b[1, piece : piece + 8]
    finish(sent)
    for h in range(head_count):
        after = carried_state(later, h)
        key = gk_part[:, cols(h)] + dot_wide(v_ref[:, cols(h)], after, 1)
        gk_ref[:, cols(h)] = key.astype(BF16)
        val = gv_part[:, cols(h)] + dot_wide(k_ref[:, cols(h)], after, 0)
        gv_ref[:, cols(h)] = val.astype(BF16)


def local(z_count, queries, key_vectors, value_vectors, out_grad, norm_gain):
    tokens, features = queries.shape
    head_count = features // DH
    block_count = tokens // BLOCK
    y_count = lax.axis_size("head")
    piece = head_count * DH // PLANE
    like = jax.ShapeDtypeStruct((tokens, features), BF16)
    vmem = pl.BlockSpec(memory_space=pltpu.VMEM)

    def scan_scratch(rows):
        return [
            pltpu.VMEM((PLANE, rows, DH), F32),
            pltpu.VMEM((PLANE, rows, DH), F32),
            pltpu.VMEM((rows, DH), F32),
            pltpu.VMEM((len(NEAR), rows, DH), F32),
            pltpu.VMEM((rows, DH), F32),
            pltpu.VMEM((len(FAR), rows, DH), F32),
            pltpu.VMEM((PLANE, piece, DH), F32),
        ]

    far_count = len(NEAR) + len(FAR)
    scan_sems = [pltpu.SemaphoreType.DMA((n,)) for n in (PLANE, PLANE, far_count, far_count, PLANE, PLANE)]
    outs = pl.pallas_call(
        functools.partial(kernel, z_count, y_count, head_count, block_count),
        out_shape=(like, like, like, jax.ShapeDtypeStruct((8, DH), F32)),
        in_specs=[vmem] * 5,
        out_specs=(vmem,) * 4,
        scratch_shapes=[
            pltpu.VMEM((head_count, DH, DH), F32),
            pltpu.VMEM((tokens, features), F32),
            pltpu.VMEM((tokens, features), BF16),
            pltpu.VMEM((tokens, features), BF16),
            pltpu.VMEM((tokens, features), F32),
            pltpu.VMEM((tokens, features), F32),
            pltpu.VMEM((PLANE, piece, DH), F32),
            pltpu.VMEM((PLANE, piece, DH), F32),
            *scan_scratch(piece),
            *scan_scratch(piece + 8),
            pltpu.VMEM((y_count, 8, tokens), F32),
            *scan_sems,
            *scan_sems,
            pltpu.SemaphoreType.DMA((y_count,)),
            pltpu.SemaphoreType.DMA((y_count,)),
        ],
        compiler_params=pltpu.CompilerParams(
            collective_id=0, has_side_effects=True, vmem_limit_bytes=48 * 1024 * 1024
        ),
        name="linear_attention_backward",
    )(queries, key_vectors, value_vectors, out_grad, norm_gain.reshape(1, features))
    return outs[0], outs[1], outs[2], outs[3][:head_count].reshape(features)


def solution(mesh):
    in_specs = (P("seq", "head"), P("seq", "head"), P("seq", "head"), P("seq", "head"), P("head"))
    out_specs = (P("seq", "head"), P("seq", "head"), P("seq", "head"), P("head"))
    body = functools.partial(local, mesh.shape["seq"] // PLANE)
    return jax.shard_map(body, mesh=mesh, in_specs=in_specs, out_specs=out_specs, check_vma=False)
```

time: 605 us -> 76.5 us (0.13)
  blocking collectives: 312 us -> 0 us
  waiting for transfers between devices: 162 us -> 0 us
  other arithmetic: 98.1 us -> 0 us
  Pallas kernels: 0 us -> 68.4 us
  between operations: 14.2 us -> 0.65 us
  matrix products: 6.28 us -> 0 us
    psum x3 -> x0, blocking collectives: 312 us -> none  [the longest x1 288 us: local(): grad_gain = lax.psum(gain_part, 'seq')]
    all_gather x2 -> x0, waiting for transfers between devices: 162 us -> none  [carried_in(): gathered = lax.all_gather(part, axis)]
    add x95 -> x0, other arithmetic: 96 us -> none  [add_pair(): return first + second]
    pallas_call x0 -> x1, Pallas kernels: none -> 68.4 us  [local(): pl.pallas_call(functools.partial(kernel, z_count, y_count, head_count, bl...]
    dot_general x12 -> x0, matrix products: 6.28 us -> none  [the longest x1 1.04 us: local(): jnp.einsum('bthd,bthe->bhde', query_blocks, grad_attention, preferred_ele...]
  transfers between devices with their start and end apart: 2 -> 0, of which waited for: 1 -> 0; matrix products, arithmetic and copies ran while one was open for 1% -> 0% of each run, Pallas kernels for 0% -> 0%
where the time goes in v1:
time: 76.5 us; the launch traced here: 76.2 us
  Pallas kernels  68.4 us (89%)
  local copies, waits for them, and re-layouts  7.16 us (9%)
    pallas_call x1, Pallas kernels, local(): pl.pallas_call(functools.partial(kernel, z_count, y_count, head_count, bl...  68.4 us
    unnamed x13, local copies, waits for them, and re-layouts  6.58 us

profile of v1, /device:TPU:1, one launch (start us, length us, event | category | flops | bytes accessed | tf_op | source)
XLA Modules:
  0.0 76.2 jit_solution(12882234153077084347)
XLA Ops:
  0.6 0.0 copy-start
  0.6 0.9 %copy-done = bf16[256,512]{1,0:T(8,128)(2,1)S(1)} copy-done((bf16[256,512]{1,0:T(8,128)(2,1)S(1)}, bf16[256,512]{1,0:T(8,128)(2,1)}, u32[]{:S(2)}) %copy-start) | copy-done | bytes 262168
  1.6 0.0 copy-start.1
  1.6 0.9 %copy-done.1 = bf16[256,512]{1,0:T(8,128)(2,1)S(1)} copy-done((bf16[256,512]{1,0:T(8,128)(2,1)S(1)}, bf16[256,512]{1,0:T(8,128)(2,1)}, u32[]{:S(2)}) %copy-start.1) | copy-done | bytes 262168
  2.5 0.0 copy-start.2
  2.5 0.9 %copy-done.2 = bf16[256,512]{1,0:T(8,128)(2,1)S(1)} copy-done((bf16[256,512]{1,0:T(8,128)(2,1)S(1)}, bf16[256,512]{1,0:T(8,128)(2,1)}, u32[]{:S(2)}) %copy-start.2) | copy-done | bytes 262168
  3.5 0.0 copy-start.3
  3.5 0.9 %copy-done.3 = bf16[256,512]{1,0:T(8,128)(2,1)S(1)} copy-done((bf16[256,512]{1,0:T(8,128)(2,1)S(1)}, bf16[256,512]{1,0:T(8,128)(2,1)}, u32[]{:S(2)}) %copy-start.3) | copy-done | bytes 262168
  4.4 0.0 copy-start.4
  4.4 0.7 copy-done.4
  5.1 68.4 %linear_attention_backward.1 = (bf16[256,512]{1,0:T(8,128)(2,1)S(1)}, bf16[256,512]{1,0:T(8,128)(2,1)S(1)}, bf16[256,512]{1,0:T(8,128)(2,1)S(1)}, f32[8,128]{1,0:T(8,128)S(1)}) custom-call(bf16[256,512]{1,0:T(8,128)(2,1)S(1)} %copy-done, bf16[256,512]{1,0:T(8,128)(2,1)S(1)} %copy-done.1, bf16[256,512]{1,0:T(8,128)(2,1)S(1)} %copy-done.2, ...), custom_call_target="tpu_custom_call" | custom-call | tf_op jit(solution)/shard_map/linear_attention_backward/pallas_call | solution.py:304
  73.5 0.6 slice_bitcast_fusion
  74.1 0.7 copy.12
  74.8 0.7 copy.13
  75.5 0.7 copy.14
Async XLA Ops:
  0.6 1.0 %copy-start = (bf16[256,512]{1,0:T(8,128)(2,1)S(1)}, bf16[256,512]{1,0:T(8,128)(2,1)}, u32[]{:S(2)}) copy-start(bf16[256,512]{1,0:T(8,128)(2,1)} %q_ref.1) | copy-start | bytes 786436
  1.6 0.9 %copy-start.1 = (bf16[256,512]{1,0:T(8,128)(2,1)S(1)}, bf16[256,512]{1,0:T(8,128)(2,1)}, u32[]{:S(2)}) copy-start(bf16[256,512]{1,0:T(8,128)(2,1)} %k_ref.1) | copy-start | bytes 786436
  2.5 0.9 %copy-start.2 = (bf16[256,512]{1,0:T(8,128)(2,1)S(1)}, bf16[256,512]{1,0:T(8,128)(2,1)}, u32[]{:S(2)}) copy-start(bf16[256,512]{1,0:T(8,128)(2,1)} %v_ref.1) | copy-start | bytes 786436
  3.5 0.9 %copy-start.3 = (bf16[256,512]{1,0:T(8,128)(2,1)S(1)}, bf16[256,512]{1,0:T(8,128)(2,1)}, u32[]{:S(2)}) copy-start(bf16[256,512]{1,0:T(8,128)(2,1)} %g_ref.1) | copy-start | bytes 786436
  4.4 0.7 copy-start.4

commit v2 on v1

v2 whole, which is shorter than its diff:
```python
import functools

import jax
import jax.numpy as jnp
from jax import lax
from jax.experimental import pallas as pl
from jax.experimental.pallas import tpu as pltpu
from jax.sharding import PartitionSpec as P

DH = 128
BLOCK = 128
PLANE = 8
NEAR = (2, -2, 1, -1)
FAR = ((4, (-2, -1, 0, 1)), (-4, (-1, 0, 1)))
EPSILON = 1e-06
CHUNKS = 2
MESH = pl.DeviceIdType.MESH
F32 = jnp.float32
BF16 = jnp.bfloat16


def dot(left, right, left_dim, right_dim):
    return lax.dot_general(
        left, right, (((left_dim,), (right_dim,)), ((), ())), preferred_element_type=F32
    )


def split(wide):
    high = wide.astype(BF16)
    low = (wide - high.astype(F32)).astype(BF16)
    return high, low


def dot_wide(left, wide, wide_dim):
    high, low = split(wide)
    return dot(left, high, 1, wide_dim) + dot(left, low, 1, wide_dim)


def kernel(
    z_count, y_count, head_count, block_count,
    q_hbm, k_hbm, v_hbm, g_hbm, gain_hbm,
    gq_ref, gk_ref, gv_ref, gg_ref,
    q_ref, k_ref, v_ref, g_ref, gain_ref,
    inner, inner_b, att, scores, grad_att, gk_part, gv_part, earlier, later,
    total_f, plane_f, step_f, near_f, window_f, far_f, stage_f,
    total_b, plane_b, step_b, near_b, window_b, far_b, stage_b,
    sums,
    fa_send, fa_recv, fb_send, fb_recv, fc_send, fc_recv,
    ba_send, ba_recv, bb_send, bb_recv, bc_send, bc_recv,
    h_send, h_recv, load_sem,
):
    loads = {}
    pairs = ((k_hbm, k_ref), (v_hbm, v_ref), (q_hbm, q_ref), (g_hbm, g_ref), (gain_hbm, gain_ref))
    for i, (source, target) in enumerate(pairs):
        loads[i] = pltpu.make_async_copy(source, target, load_sem.at[i])
        if i < 2:
            loads[i].start()

    seq = lax.axis_index("seq")
    y = lax.axis_index("head")
    z = lax.div(seq, PLANE)
    p = lax.rem(seq, PLANE)
    heads_each = head_count // CHUNKS
    piece = heads_each * DH // PLANE
    model_width = y_count * head_count * DH

    def in_plane(offset):
        return lax.rem(p + offset, PLANE)

    def in_column(offset):
        return lax.rem(z + offset, z_count)

    def seq_of(at_z, at_p):
        return at_z * PLANE + at_p

    hops = NEAR + tuple(d for d, _ in FAR)
    barrier = pltpu.get_barrier_semaphore()
    for k in range(1, PLANE):
        pl.semaphore_signal(barrier, inc=1, device_id=(seq_of(z, in_plane(k)), y), device_id_type=MESH)
    for d in hops:
        pl.semaphore_signal(barrier, inc=1, device_id=(seq_of(in_column(d % z_count), p), y), device_id_type=MESH)
    for k in range(1, y_count):
        pl.semaphore_signal(barrier, inc=1, device_id=(seq, lax.rem(y + k, y_count)), device_id_type=MESH)

    for i in range(2, len(pairs)):
        loads[i].start()
    unsent = []

    def remote(source, target, send, recv, seq_to, y_to):
        copy = pltpu.make_async_remote_copy(
            src_ref=source, dst_ref=target, send_sem=send, recv_sem=recv,
            device_id=(seq_to, y_to), device_id_type=MESH,
        )
        copy.start()
        unsent.append(copy)
        return copy

    def arrived(copies):
        for copy in copies:
            copy.wait_recv()

    row = lax.broadcasted_iota(jnp.int32, (BLOCK, BLOCK), 0)
    col = lax.broadcasted_iota(jnp.int32, (BLOCK, BLOCK), 1)
    causal = row >= col
    part_rows = DH // PLANE * heads_each
    halves = DH // part_rows if part_rows < DH else 1

    def at(ref, b, h):
        return ref[b * BLOCK : (b + 1) * BLOCK, h * DH : (h + 1) * DH]

    def cols(h):
        return slice(h * DH, (h + 1) * DH)

    def put_total(total, h, value):
        c, place = divmod(h, heads_each)
        for i in range(halves):
            total[c, place * halves + i, 0:piece] = value[i * piece : (i + 1) * piece]

    def carried_state(ref, h):
        c, place = divmod(h, heads_each)
        return jnp.concatenate([ref[c, place * halves + i] for i in range(halves)], axis=0)

    class Scan:
        def __init__(self, refs, target, sems, reverse):
            self.total, self.plane, self.step, self.near, self.window, self.far, self.stage = refs
            self.target = target
            self.a_send, self.a_recv, self.b_send, self.b_recv, self.c_send, self.c_recv = sems
            self.reverse = reverse
            self.flying = {}
            self.before = {}

        def rows(self, c):
            return piece + 8 if self.reverse and c == CHUNKS - 1 else piece

        def around(self, c, place, n):
            if place == 0:
                return self.step[c, 0:n]
            return self.near[c, NEAR.index(-place), 0:n]

        def collect(self, c, distance, places):
            n = self.rows(c)
            here = z_count - 1 - z if self.reverse else z
            target = lax.rem(here + distance % z_count, z_count)
            state = None
            for place in places:
                behind = (distance - place) % z_count
                value = self.around(c, place, n)
                kept = jnp.where(target >= behind, value[:piece], 0.0)
                state = kept if state is None else state + kept
            if n == piece:
                return state
            gain = self.around(c, places[0], n)[piece:]
            for place in places[1:]:
                gain = gain + self.around(c, place, n)[piece:]
            return jnp.concatenate([state, gain], axis=0)

        def plane_out(self, c):
            n = self.rows(c)
            self.flying[c] = []
            for k in (4, 3, 5, 2, 6, 1, 7):
                to = in_plane(k)
                self.flying[c].append(remote(
                    self.total.at[c, to, 0:n], self.plane.at[c, p, 0:n],
                    self.a_send.at[c, k], self.a_recv.at[c, k], seq_of(z, to), y,
                ))
            self.plane[c, p] = self.total[c, p]

        def column_out(self, c, i, distance, source, target):
            to = in_column((-distance if self.reverse else distance) % z_count)
            return remote(source, target, self.b_send.at[c, i], self.b_recv.at[c, i], seq_of(to, p), y)

        def near_out(self, c):
            n = self.rows(c)
            arrived(self.flying[c])
            value = self.plane[c, 0, 0:n]
            for s in range(1, PLANE):
                value = value + self.plane[c, s, 0:n]
            self.step[c, 0:n] = value
            self.flying[c] = [
                self.column_out(c, i, d, self.step.at[c, 0:n], self.near.at[c, i, 0:n])
                for i, d in enumerate(NEAR)
            ]

        def far_out(self, c):
            n = self.rows(c)
            arrived(self.flying[c])
            self.flying[c] = []
            for i, (d, places) in enumerate(FAR):
                self.window[c, i, 0:n] = self.collect(c, d, places)
                self.flying[c].append(self.column_out(
                    c, len(NEAR) + i, d, self.window.at[c, i, 0:n], self.far.at[c, i, 0:n]
                ))
            self.before[c] = self.collect(c, 0, tuple(-d for d in NEAR))

        def plane_back(self, c):
            arrived(self.flying[c])
            value = self.before[c][:piece]
            for i in range(len(FAR)):
                value = value + self.far[c, i, 0:piece]
            order = range(PLANE - 1, -1, -1) if self.reverse else range(PLANE)
            for s in order:
                self.stage[c, s] = value
                value = value + self.plane[c, s, 0:piece]
            self.flying[c] = []
            for k in (4, 3, 5, 2, 6, 1, 7):
                to = in_plane(k)
                self.flying[c].append(remote(
                    self.stage.at[c, to], self.target.at[c, p],
                    self.c_send.at[c, k], self.c_recv.at[c, k], seq_of(z, to), y,
                ))
            self.target[c, p] = self.stage[c, p]

        def landed(self, c):
            arrived(self.flying[c])

    forward = Scan(
        (total_f, plane_f, step_f, near_f, window_f, far_f, stage_f), earlier,
        (fa_send, fa_recv, fb_send, fb_recv, fc_send, fc_recv), False,
    )
    backward = Scan(
        (total_b, plane_b, step_b, near_b, window_b, far_b, stage_b), later,
        (ba_send, ba_recv, bb_send, bb_recv, bc_send, bc_recv), True,
    )

    def of_chunk(c):
        return range(c * heads_each, (c + 1) * heads_each)

    loads[0].wait()
    loads[1].wait()
    for c in range(CHUNKS):
        for h in of_chunk(c):
            first = dot(at(k_ref, 0, h), at(v_ref, 0, h), 0, 0)
            second = dot(at(k_ref, 1, h), at(v_ref, 1, h), 0, 0)
            inner[h] = first
            put_total(total_f, h, first + second)
        if c == 0:
            pl.semaphore_wait(barrier, PLANE - 1 + len(hops) + y_count - 1)
        forward.plane_out(c)

    def inside(h):
        for b in range(block_count):
            products = dot(at(q_ref, b, h), at(k_ref, b, h), 1, 1)
            kept = jnp.where(causal, products, 0.0).astype(BF16)
            scores[b * BLOCK : (b + 1) * BLOCK, cols(h)] = kept
            value = dot(kept, at(v_ref, b, h), 1, 0)
            if b == 1:
                value = value + dot_wide(at(q_ref, b, h), inner[h], 0)
            att[b * BLOCK : (b + 1) * BLOCK, cols(h)] = value

    loads[2].wait()
    for h in range(head_count // 2):
        inside(h)
    for c in range(CHUNKS):
        forward.near_out(c)
    for h in range(head_count // 2, head_count):
        inside(h)
    for c in range(CHUNKS):
        forward.far_out(c)
    for c in range(CHUNKS):
        forward.plane_back(c)
    loads[3].wait()
    loads[4].wait()

    tokens = block_count * BLOCK
    squares = jnp.zeros((tokens, DH), F32)
    weighted = jnp.zeros((tokens, DH), F32)
    for c in range(CHUNKS):
        forward.landed(c)
        for h in of_chunk(c):
            value = att[:, cols(h)] + dot_wide(q_ref[:, cols(h)], carried_state(earlier, h), 0)
            att[:, cols(h)] = value
            squares = squares + value * value
            weighted = weighted + gain_ref[:, cols(h)] * g_ref[:, cols(h)].astype(F32) * value
    square_row = jnp.sum(squares.T, axis=0, keepdims=True)
    weighted_row = jnp.sum(weighted.T, axis=0, keepdims=True)
    line = lax.broadcasted_iota(jnp.int32, (8, tokens), 0)
    sums[0] = jnp.where(line == 0, square_row, jnp.where(line == 1, weighted_row, 0.0))
    sent = []
    for k in (4, 3, 5, 2, 6, 1, 7):
        to = lax.rem(y + k, y_count)
        sent.append(remote(sums.at[0], sums.at[k], h_send.at[k], h_recv.at[k], seq, to))
    arrived(sent)
    whole = sums[0]
    for k in range(1, y_count):
        whole = whole + sums[k]
    inverse_row = 1.0 / jnp.sqrt(whole[0:1] / model_width + EPSILON)
    pull_row = inverse_row * inverse_row * inverse_row * whole[1:2] / model_width
    inverse = jnp.broadcast_to(inverse_row, (DH, tokens)).T
    pull = jnp.broadcast_to(pull_row, (DH, tokens)).T

    gain_line = lax.broadcasted_iota(jnp.int32, (8, DH), 0)
    gain_part = jnp.zeros((8, DH), F32)
    for c in range(CHUNKS):
        for h in of_chunk(c):
            value = att[:, cols(h)]
            scaled = g_ref[:, cols(h)].astype(F32) * inverse
            gain_sum = jnp.sum(scaled * value, axis=0, keepdims=True)
            gain_part = jnp.where(gain_line == h, gain_sum, gain_part)
            grad = (gain_ref[:, cols(h)] * scaled - value * pull).astype(BF16)
            grad_att[:, cols(h)] = grad
            first = dot(at(q_ref, 0, h), grad[:BLOCK], 0, 0)
            second = dot(at(q_ref, 1, h), grad[BLOCK:], 0, 0)
            inner_b[h] = second
            put_total(total_b, h, first + second)
        if c == CHUNKS - 1:
            for s in range(PLANE):
                total_b[c, s, piece : piece + 8] = gain_part
        backward.plane_out(c)

    def inside_grads(h):
        state = carried_state(earlier, h)
        for b in range(block_count):
            rows = slice(b * BLOCK, (b + 1) * BLOCK)
            grad = grad_att[rows, cols(h)]
            products = dot(grad, at(v_ref, b, h), 1, 1)
            grad_scores = jnp.where(causal, products, 0.0).astype(BF16)
            here = state + inner[h] if b == 1 else state
            value = dot(grad_scores, at(k_ref, b, h), 1, 0) + dot_wide(grad, here, 1)
            gq_ref[rows, cols(h)] = value.astype(BF16)
            key = dot(grad_scores, at(q_ref, b, h), 0, 0)
            val = dot(scores[rows, cols(h)], grad, 0, 0)
            if b == 0:
                key = key + dot_wide(at(v_ref, b, h), inner_b[h], 1)
                val = val + dot_wide(at(k_ref, b, h), inner_b[h], 0)
            gk_part[rows, cols(h)] = key
            gv_part[rows, cols(h)] = val

    for h in range(head_count // 2):
        inside_grads(h)
    for c in range(CHUNKS):
        backward.near_out(c)
    for h in range(head_count // 2, 3 * head_count // 4):
        inside_grads(h)
    for c in range(CHUNKS):
        backward.far_out(c)
    for h in range(3 * head_count // 4, head_count):
        inside_grads(h)
    for c in range(CHUNKS):
        backward.plane_back(c)
    last = CHUNKS - 1
    gain_rows = slice(piece, piece + 8)
    whole_gain = backward.before[last][gain_rows] + step_b[last, gain_rows]
    for i in range(len(FAR)):
        whole_gain = whole_gain + far_b[last, i, gain_rows]
    for h in range(head_count):
        gg_ref[:, cols(h)] = whole_gain[h : h + 1]
    for c in range(CHUNKS):
        backward.landed(c)
        for h in of_chunk(c):
            after = carried_state(later, h)
            key = gk_part[:, cols(h)] + dot_wide(v_ref[:, cols(h)], after, 1)
            gk_ref[:, cols(h)] = key.astype(BF16)
            val = gv_part[:, cols(h)] + dot_wide(k_ref[:, cols(h)], after, 0)
            gv_ref[:, cols(h)] = val.astype(BF16)
    for copy in unsent:
        copy.wait_send()


def write_out(a_ref, b_ref, c_ref, d_ref, a_hbm, b_hbm, c_hbm, d_hbm, sem):
    copies = []
    pairs = ((a_ref, a_hbm), (b_ref, b_hbm), (c_ref, c_hbm), (d_ref, d_hbm))
    for i, (source, target) in enumerate(pairs):
        copies.append(pltpu.make_async_copy(source, target, sem.at[i]))
        copies[-1].start()
    for copy in copies:
        copy.wait()


def local(z_count, queries, key_vectors, value_vectors, out_grad, norm_gain):
    tokens, features = queries.shape
    head_count = features // DH
    block_count = tokens // BLOCK
    y_count = lax.axis_size("head")
    piece = head_count // CHUNKS * DH // PLANE
    like = jax.ShapeDtypeStruct((tokens, features), BF16)
    shapes = (like, like, like, jax.ShapeDtypeStruct((1, features), F32))
    vmem = pl.BlockSpec(memory_space=pltpu.VMEM)
    hbm = pl.BlockSpec(memory_space=pltpu.HBM)

    def scan_scratch(rows):
        return [
            pltpu.VMEM((CHUNKS, PLANE, rows, DH), F32),
            pltpu.VMEM((CHUNKS, PLANE, rows, DH), F32),
            pltpu.VMEM((CHUNKS, rows, DH), F32),
            pltpu.VMEM((CHUNKS, len(NEAR), rows, DH), F32),
            pltpu.VMEM((CHUNKS, len(FAR), rows, DH), F32),
            pltpu.VMEM((CHUNKS, len(FAR), rows, DH), F32),
            pltpu.VMEM((CHUNKS, PLANE, piece, DH), F32),
        ]

    z_copies = len(NEAR) + len(FAR)
    scan_sems = [
        pltpu.SemaphoreType.DMA((CHUNKS, n)) for n in (PLANE, PLANE, z_copies, z_copies, PLANE, PLANE)
    ]
    operands = (queries, key_vectors, value_vectors, out_grad, norm_gain.reshape(1, features))
    results = pl.pallas_call(
        functools.partial(kernel, z_count, y_count, head_count, block_count),
        out_shape=shapes,
        in_specs=[hbm] * 5,
        out_specs=(vmem,) * 4,
        scratch_shapes=[
            *[pltpu.VMEM((tokens, features), BF16)] * 4,
            pltpu.VMEM((1, features), F32),
            pltpu.VMEM((head_count, DH, DH), F32),
            pltpu.VMEM((head_count, DH, DH), F32),
            pltpu.VMEM((tokens, features), F32),
            pltpu.VMEM((tokens, features), BF16),
            pltpu.VMEM((tokens, features), BF16),
            pltpu.VMEM((tokens, features), F32),
            pltpu.VMEM((tokens, features), F32),
            pltpu.VMEM((CHUNKS, PLANE, piece, DH), F32),
            pltpu.VMEM((CHUNKS, PLANE, piece, DH), F32),
            *scan_scratch(piece),
            *scan_scratch(piece + 8),
            pltpu.VMEM((y_count, 8, tokens), F32),
            *scan_sems,
            *scan_sems,
            pltpu.SemaphoreType.DMA((y_count,)),
            pltpu.SemaphoreType.DMA((y_count,)),
            pltpu.SemaphoreType.DMA((5,)),
        ],
        compiler_params=pltpu.CompilerParams(
            collective_id=0, has_side_effects=True, vmem_limit_bytes=32 * 1024 * 1024
        ),
        name="linear_attention_backward",
    )(*[pltpu.with_memory_space_constraint(x, pltpu.HBM) for x in operands])
    outs = pl.pallas_call(
        write_out,
        out_shape=shapes,
        in_specs=[vmem] * 4,
        out_specs=(hbm,) * 4,
        scratch_shapes=[pltpu.SemaphoreType.DMA((4,))],
        name="write_out",
    )(*[pltpu.with_memory_space_constraint(x, pltpu.VMEM) for x in results])
    return outs[0], outs[1], outs[2], outs[3].reshape(features)


def solution(mesh):
    in_specs = (P("seq", "head"), P("seq", "head"), P("seq", "head"), P("seq", "head"), P("head"))
    out_specs = (P("seq", "head"), P("seq", "head"), P("seq", "head"), P("head"))
    body = functools.partial(local, mesh.shape["seq"] // PLANE)
    return jax.shard_map(body, mesh=mesh, in_specs=in_specs, out_specs=out_specs, check_vma=False)
```

time: 76.5 us -> 63.7 us (0.83)
  local copies, waits for them, and re-layouts: 7.16 us -> 0 us
  Pallas kernels: 68.4 us -> 62.9 us
    unnamed x13 -> x0, local copies, waits for them, and re-layouts: 6.58 us -> none
    pallas_call x1, Pallas kernels: 68.4 us -> 62 us  [local(): pl.pallas_call(functools.partial(kernel, z_count, y_count, head_count, bl...]
    pallas_call x0 -> x1, Pallas kernels: none -> 0.91 us  [local(): pl.pallas_call(write_out, out_shape=shapes, in_specs=[vmem] * 4, out_spec...]
where the time goes in v2:
time: 63.7 us; the launch traced here: 63.6 us
  Pallas kernels  62.9 us (99%)
  between operations  0.64 us (1%)
    pallas_call x1, Pallas kernels, local(): pl.pallas_call(functools.partial(kernel, z_count, y_count, head_count, bl...  62 us

profile of v2, /device:TPU:1, one launch (start us, length us, event | category | flops | bytes accessed | tf_op | source)
XLA Modules:
  0.0 63.6 jit_solution(2944159690209978149)
XLA Ops:
  0.6 62.0 %linear_attention_backward.1 = (bf16[256,512]{1,0:T(8,128)(2,1)S(1)}, bf16[256,512]{1,0:T(8,128)(2,1)S(1)}, bf16[256,512]{1,0:T(8,128)(2,1)S(1)}, f32[1,512]{1,0:T(1,128)S(1)}) custom-call(bf16[256,512]{1,0:T(8,128)(2,1)} %q_hbm.1, bf16[256,512]{1,0:T(8,128)(2,1)} %k_hbm.1, bf16[256,512]{1,0:T(8,128)(2,1)} %v_hbm.1, bf16[256,512]{1,0:T(8,128)(2,1)} %g_hbm.1, ...), custom_call_target="tpu_custom_call" | custom-call | tf_op jit(solution)/shard_map/linear_attention_backward/pallas_call | solution.py:396
  62.7 0.9 %write_out.1 = (bf16[256,512]{1,0:T(8,128)(2,1)}, bf16[256,512]{1,0:T(8,128)(2,1)}, bf16[256,512]{1,0:T(8,128)(2,1)}, f32[1,512]{1,0:T(1,128)}) custom-call(bf16[256,512]{1,0:T(8,128)(2,1)S(1)} %get-tuple-element.12.a_ref, bf16[256,512]{1,0:T(8,128)(2,1)S(1)} %get-tuple-element.13.b_ref, bf16[256,512]{1,0:T(8,128)(2,1)S(1)} %get-tuple-element.14.c_ref, ...), custom_call_target="tpu_custom_call" | custom-call | tf_op jit(solution)/shard_map/write_out/pallas_call | solution.py:427

commit v3 on v2

--- a/solution.py
+++ b/solution.py
@@ -45,9 +45,7 @@
     total_f, plane_f, step_f, near_f, window_f, far_f, stage_f,
     total_b, plane_b, step_b, near_b, window_b, far_b, stage_b,
     sums,
-    fa_send, fa_recv, fb_send, fb_recv, fc_send, fc_recv,
-    ba_send, ba_recv, bb_send, bb_recv, bc_send, bc_recv,
-    h_send, h_recv, load_sem,
+    f_send, f_recv, b_send, b_recv, h_send, h_recv, load_sem,
 ):
     loads = {}
     pairs = ((k_hbm, k_ref), (v_hbm, v_ref), (q_hbm, q_ref), (g_hbm, g_ref), (gain_hbm, gain_ref))
@@ -92,12 +90,13 @@
             device_id=(seq_to, y_to), device_id_type=MESH,
         )
         copy.start()
-        unsent.append(copy)
-        return copy
-
-    def arrived(copies):
-        for copy in copies:
-            copy.wait_recv()
+
+    def bytes_of(ref, sem):
+        pltpu.make_async_copy(ref, ref, sem).wait()
+
+    def flying(ref, send, recv):
+        unsent.append((ref, send))
+        return ref, recv
 
     row = lax.broadcasted_iota(jnp.int32, (BLOCK, BLOCK), 0)
     col = lax.broadcasted_iota(jnp.int32, (BLOCK, BLOCK), 1)
@@ -124,10 +123,13 @@
         def __init__(self, refs, target, sems, reverse):
             self.total, self.plane, self.step, self.near, self.window, self.far, self.stage = refs
             self.target = target
-            self.a_send, self.a_recv, self.b_send, self.b_recv, self.c_send, self.c_recv = sems
+            self.send, self.recv = sems
             self.reverse = reverse
             self.flying = {}
             self.before = {}
+
+        def fly(self, c, phase, ref):
+            self.flying[c] = flying(ref, self.send.at[c, phase], self.recv.at[c, phase])
 
         def rows(self, c):
             return piece + 8 if self.reverse and c == CHUNKS - 1 else piece
@@ -156,44 +158,41 @@
 
         def plane_out(self, c):
             n = self.rows(c)
-            self.flying[c] = []
             for k in (4, 3, 5, 2, 6, 1, 7):
                 to = in_plane(k)
-                self.flying[c].append(remote(
+                remote(
                     self.total.at[c, to, 0:n], self.plane.at[c, p, 0:n],
-                    self.a_send.at[c, k], self.a_recv.at[c, k], seq_of(z, to), y,
-                ))
+                    self.send.at[c, 0], self.recv.at[c, 0], seq_of(z, to), y,
+                )
+            self.fly(c, 0, self.plane.at[c, 0 : PLANE - 1, 0:n])
             self.plane[c, p] = self.total[c, p]
 
-        def column_out(self, c, i, distance, source, target):
+        def column_out(self, c, phase, distance, source, target):
             to = in_column((-distance if self.reverse else distance) % z_count)
-            return remote(source, target, self.b_send.at[c, i], self.b_recv.at[c, i], seq_of(to, p), y)
+            remote(source, target, self.send.at[c, phase], self.recv.at[c, phase], seq_of(to, p), y)
 
         def near_out(self, c):
             n = self.rows(c)
-            arrived(self.flying[c])
+            bytes_of(*self.flying[c])
             value = self.plane[c, 0, 0:n]
             for s in range(1, PLANE):
                 value = value + self.plane[c, s, 0:n]
             self.step[c, 0:n] = value
-            self.flying[c] = [
-                self.column_out(c, i, d, self.step.at[c, 0:n], self.near.at[c, i, 0:n])
-                for i, d in enumerate(NEAR)
-            ]
+            for i, d in enumerate(NEAR):
+                self.column_out(c, 1, d, self.step.at[c, 0:n], self.near.at[c, i, 0:n])
+            self.fly(c, 1, self.near.at[c, :, 0:n])
 
         def far_out(self, c):
             n = self.rows(c)
-            arrived(self.flying[c])
-            self.flying[c] = []
+            bytes_of(*self.flying[c])
             for i, (d, places) in enumerate(FAR):
                 self.window[c, i, 0:n] = self.collect(c, d, places)
-                self.flying[c].append(self.column_out(
-                    c, len(NEAR) + i, d, self.window.at[c, i, 0:n], self.far.at[c, i, 0:n]
-                ))
+                self.column_out(c, 2, d, self.window.at[c, i, 0:n], self.far.at[c, i, 0:n])
+            self.fly(c, 2, self.far.at[c, :, 0:n])
             self.before[c] = self.collect(c, 0, tuple(-d for d in NEAR))
 
         def plane_back(self, c):
-            arrived(self.flying[c])
+            bytes_of(*self.flying[c])
             value = self.before[c][:piece]
             for i in range(len(FAR)):
                 value = value + self.far[c, i, 0:piece]
@@ -201,25 +200,25 @@
             for s in order:
                 self.stage[c, s] = value
                 value = value + self.plane[c, s, 0:piece]
-            self.flying[c] = []
             for k in (4, 3, 5, 2, 6, 1, 7):
                 to = in_plane(k)
-                self.flying[c].append(remote(
+                remote(
                     self.stage.at[c, to], self.target.at[c, p],
-                    self.c_send.at[c, k], self.c_recv.at[c, k], seq_of(z, to), y,
-                ))
+                    self.send.at[c, 3], self.recv.at[c, 3], seq_of(z, to), y,
+                )
+            self.fly(c, 3, self.target.at[c, 0 : PLANE - 1])
             self.target[c, p] = self.stage[c, p]
 
         def landed(self, c):
-            arrived(self.flying[c])
+            bytes_of(*self.flying[c])
 
     forward = Scan(
         (total_f, plane_f, step_f, near_f, window_f, far_f, stage_f), earlier,
-        (fa_send, fa_recv, fb_send, fb_recv, fc_send, fc_recv), False,
+        (f_send, f_recv), False,
     )
     backward = Scan(
         (total_b, plane_b, step_b, near_b, window_b, far_b, stage_b), later,
-        (ba_send, ba_recv, bb_send, bb_recv, bc_send, bc_recv), True,
+        (b_send, b_recv), True,
     )
 
     def of_chunk(c):
@@ -273,13 +272,11 @@
             weighted = weighted + gain_ref[:, cols(h)] * g_ref[:, cols(h)].astype(F32) * value
     square_row = jnp.sum(squares.T, axis=0, keepdims=True)
     weighted_row = jnp.sum(weighted.T, axis=0, keepdims=True)
-    line = lax.broadcasted_iota(jnp.int32, (8, tokens), 0)
-    sums[0] = jnp.where(line == 0, square_row, jnp.where(line == 1, weighted_row, 0.0))
-    sent = []
+    sums[0, 0:1] = square_row
+    sums[0, 1:2] = weighted_row
     for k in (4, 3, 5, 2, 6, 1, 7):
-        to = lax.rem(y + k, y_count)
-        sent.append(remote(sums.at[0], sums.at[k], h_send.at[k], h_recv.at[k], seq, to))
-    arrived(sent)
+        remote(sums.at[0], sums.at[k], h_send, h_recv, seq, lax.rem(y + k, y_count))
+    bytes_of(*flying(sums.at[1:y_count], h_send, h_recv))
     whole = sums[0]
     for k in range(1, y_count):
         whole = whole + sums[k]
@@ -352,8 +349,8 @@
             gk_ref[:, cols(h)] = key.astype(BF16)
             val = gv_part[:, cols(h)] + dot_wide(k_ref[:, cols(h)], after, 0)
             gv_ref[:, cols(h)] = val.astype(BF16)
-    for copy in unsent:
-        copy.wait_send()
+    for ref, sem in unsent:
+        bytes_of(ref, sem)
 
 
 def write_out(a_ref, b_ref, c_ref, d_ref, a_hbm, b_hbm, c_hbm, d_hbm, sem):
@@ -388,10 +385,6 @@
             pltpu.VMEM((CHUNKS, PLANE, piece, DH), F32),
         ]
 
-    z_copies = len(NEAR) + len(FAR)
-    scan_sems = [
-        pltpu.SemaphoreType.DMA((CHUNKS, n)) for n in (PLANE, PLANE, z_copies, z_copies, PLANE, PLANE)
-    ]
     operands = (queries, key_vectors, value_vectors, out_grad, norm_gain.reshape(1, features))
     results = pl.pallas_call(
         functools.partial(kernel, z_count, y_count, head_count, block_count),
@@ -412,11 +405,10 @@
             pltpu.VMEM((CHUNKS, PLANE, piece, DH), F32),
             *scan_scratch(piece),
             *scan_scratch(piece + 8),
-            pltpu.VMEM((y_count, 8, tokens), F32),
-            *scan_sems,
-            *scan_sems,
-            pltpu.SemaphoreType.DMA((y_count,)),
-            pltpu.SemaphoreType.DMA((y_count,)),
+            pltpu.VMEM((y_count, 2, tokens), F32),
+            *[pltpu.SemaphoreType.DMA((CHUNKS, 4))] * 4,
+            pltpu.SemaphoreType.DMA,
+            pltpu.SemaphoreType.DMA,
             pltpu.SemaphoreType.DMA((5,)),
         ],
         compiler_params=pltpu.CompilerParams(

time: 63.7 us -> 62 us (0.973)
  Pallas kernels: 62.9 us -> 61.2 us
    pallas_call x1, Pallas kernels: 62 us -> 60.3 us  [local(): pl.pallas_call(functools.partial(kernel, z_count, y_count, head_count, bl...]
where the time goes in v3:
time: 62 us; the launch traced here: 61.9 us
  Pallas kernels  61.2 us (99%)
  between operations  0.64 us (1%)
    pallas_call x1, Pallas kernels, local(): pl.pallas_call(functools.partial(kernel, z_count, y_count, head_count, bl...  60.3 us

profile of v3, /device:TPU:1, one launch (start us, length us, event | category | flops | bytes accessed | tf_op | source)
XLA Modules:
  0.0 61.9 jit_solution(3044908022955238760)
XLA Ops:
  0.6 60.3 %linear_attention_backward.1 = (bf16[256,512]{1,0:T(8,128)(2,1)S(1)}, bf16[256,512]{1,0:T(8,128)(2,1)S(1)}, bf16[256,512]{1,0:T(8,128)(2,1)S(1)}, f32[1,512]{1,0:T(1,128)S(1)}) custom-call(bf16[256,512]{1,0:T(8,128)(2,1)} %q_hbm.1, bf16[256,512]{1,0:T(8,128)(2,1)} %k_hbm.1, bf16[256,512]{1,0:T(8,128)(2,1)} %v_hbm.1, bf16[256,512]{1,0:T(8,128)(2,1)} %g_hbm.1, ...), custom_call_target="tpu_custom_call" | custom-call | tf_op jit(solution)/shard_map/linear_attention_backward/pallas_call | solution.py:389
  61.0 0.9 %write_out.1 = (bf16[256,512]{1,0:T(8,128)(2,1)}, bf16[256,512]{1,0:T(8,128)(2,1)}, bf16[256,512]{1,0:T(8,128)(2,1)}, f32[1,512]{1,0:T(1,128)}) custom-call(bf16[256,512]{1,0:T(8,128)(2,1)S(1)} %get-tuple-element.12.a_ref, bf16[256,512]{1,0:T(8,128)(2,1)S(1)} %get-tuple-element.13.b_ref, bf16[256,512]{1,0:T(8,128)(2,1)S(1)} %get-tuple-element.14.c_ref, ...), custom_call_target="tpu_custom_call" | custom-call | tf_op jit(solution)/shard_map/write_out/pallas_call | solution.py:419

commit v4 on v3

--- a/solution.py
+++ b/solution.py
@@ -13,7 +13,7 @@
 NEAR = (2, -2, 1, -1)
 FAR = ((4, (-2, -1, 0, 1)), (-4, (-1, 0, 1)))
 EPSILON = 1e-06
-CHUNKS = 2
+CHUNKS = 4
 MESH = pl.DeviceIdType.MESH
 F32 = jnp.float32
 BF16 = jnp.bfloat16
@@ -73,12 +73,15 @@
 
     hops = NEAR + tuple(d for d, _ in FAR)
     barrier = pltpu.get_barrier_semaphore()
-    for k in range(1, PLANE):
+    farthest_first = (4, 3, 5, 2, 6, 1, 7)
+    for d in sorted(hops, key=abs, reverse=True):
+        to = seq_of(in_column(d % z_count), p)
+        pl.semaphore_signal(barrier, inc=1, device_id=(to, y), device_id_type=MESH)
+    for k in farthest_first:
+        to = lax.rem(y + k, y_count)
+        pl.semaphore_signal(barrier, inc=1, device_id=(seq, to), device_id_type=MESH)
+    for k in farthest_first:
         pl.semaphore_signal(barrier, inc=1, device_id=(seq_of(z, in_plane(k)), y), device_id_type=MESH)
-    for d in hops:
-        pl.semaphore_signal(barrier, inc=1, device_id=(seq_of(in_column(d % z_count), p), y), device_id_type=MESH)
-    for k in range(1, y_count):
-        pl.semaphore_signal(barrier, inc=1, device_id=(seq, lax.rem(y + k, y_count)), device_id_type=MESH)
 
     for i in range(2, len(pairs)):
         loads[i].start()
@@ -158,7 +161,7 @@
 
         def plane_out(self, c):
             n = self.rows(c)
-            for k in (4, 3, 5, 2, 6, 1, 7):
+            for k in (1, 7, 2, 6, 3, 5, 4):
                 to = in_plane(k)
                 remote(
                     self.total.at[c, to, 0:n], self.plane.at[c, p, 0:n],
@@ -200,7 +203,7 @@
             for s in order:
                 self.stage[c, s] = value
                 value = value + self.plane[c, s, 0:piece]
-            for k in (4, 3, 5, 2, 6, 1, 7):
+            for k in (1, 7, 2, 6, 3, 5, 4):
                 to = in_plane(k)
                 remote(
                     self.stage.at[c, to], self.target.at[c, p],
@@ -274,7 +277,7 @@
     weighted_row = jnp.sum(weighted.T, axis=0, keepdims=True)
     sums[0, 0:1] = square_row
     sums[0, 1:2] = weighted_row
-    for k in (4, 3, 5, 2, 6, 1, 7):
+    for k in farthest_first:
         remote(sums.at[0], sums.at[k], h_send, h_recv, seq, lax.rem(y + k, y_count))
     bytes_of(*flying(sums.at[1:y_count], h_send, h_recv))
     whole = sums[0]

time: 62 us -> 61 us (0.984)
  Pallas kernels: 61.2 us -> 60.2 us
    pallas_call x1, Pallas kernels: 60.3 us -> 59.3 us  [local(): pl.pallas_call(functools.partial(kernel, z_count, y_count, head_count, bl...]
where the time goes in v4:
time: 61 us; the launch traced here: 60.8 us
  Pallas kernels  60.2 us (99%)
  between operations  0.64 us (1%)
    pallas_call x1, Pallas kernels, local(): pl.pallas_call(functools.partial(kernel, z_count, y_count, head_count, bl...  59.3 us

profile of v4, /device:TPU:1, one launch (start us, length us, event | category | flops | bytes accessed | tf_op | source)
XLA Modules:
  0.0 60.8 jit_solution(10134881520499459792)
XLA Ops:
  0.6 59.3 %linear_attention_backward.1 = (bf16[256,512]{1,0:T(8,128)(2,1)S(1)}, bf16[256,512]{1,0:T(8,128)(2,1)S(1)}, bf16[256,512]{1,0:T(8,128)(2,1)S(1)}, f32[1,512]{1,0:T(1,128)S(1)}) custom-call(bf16[256,512]{1,0:T(8,128)(2,1)} %q_hbm.1, bf16[256,512]{1,0:T(8,128)(2,1)} %k_hbm.1, bf16[256,512]{1,0:T(8,128)(2,1)} %v_hbm.1, bf16[256,512]{1,0:T(8,128)(2,1)} %g_hbm.1, ...), custom_call_target="tpu_custom_call" | custom-call | tf_op jit(solution)/shard_map/linear_attention_backward/pallas_call | solution.py:392
  59.9 0.9 %write_out.1 = (bf16[256,512]{1,0:T(8,128)(2,1)}, bf16[256,512]{1,0:T(8,128)(2,1)}, bf16[256,512]{1,0:T(8,128)(2,1)}, f32[1,512]{1,0:T(1,128)}) custom-call(bf16[256,512]{1,0:T(8,128)(2,1)S(1)} %get-tuple-element.12.a_ref, bf16[256,512]{1,0:T(8,128)(2,1)S(1)} %get-tuple-element.13.b_ref, bf16[256,512]{1,0:T(8,128)(2,1)S(1)} %get-tuple-element.14.c_ref, ...), custom_call_target="tpu_custom_call" | custom-call | tf_op jit(solution)/shard_map/write_out/pallas_call | solution.py:422
